TPU v7x, 256 devices: a whole 4x4x8 slice. The times are simulated.
256 devices in a mesh: wide: 16 (over y_hi, x, core), narrow: 16 (over z, y_lo).
Axes of the slice: x: 4, y: 4 (y_hi: 2, y_lo: 2; y = y_hi * 2 + y_lo), z: 8, core: 2. Of those that a mesh axis runs over, the one named last changes fastest.
Arguments:
- documents: bfloat16 [16384, 768], P('wide'), may hold values from -8 to 8
- label_weight: bfloat16 [32768, 768], P(('wide', 'narrow')), may hold values from -1 to 1
- sample_ids: int32 [32768], P(('wide', 'narrow')), may hold values from 0 to 2812280, as said below
- positive_cols: int32 [16384, 4], P('wide'), may hold values from 0 to 32767
- up_weight: bfloat16 [768, 3072], P(None, 'narrow'), may hold values from -0.21875 to 0.21875
- down_weight: bfloat16 [3072, 768], P('narrow'), may hold values from -0.109375 to 0.109375
Outputs:
- label_grad: float32 [32768, 768], P(('wide', 'narrow'))
- up_grad: float32 [768, 3072], P('wide', 'narrow')
- down_grad: float32 [3072, 768], P('narrow', 'wide')
Inputs may be any that keep to these rules, and one draw needn't show every extreme that they name: `sample_ids`: frequency ranks (0 is the most frequent of 2812281 labels), not falling along the sampled columns; frequent ranks repeat.
All inputs are finite; a program needn't handle non-finite values.
Results may differ from a plain program's by a relative error of at most 0.01.
Values may be sent and summed in bfloat16 or wider, within the bound.
No kernel may reach another device: no remote copies, remote signals or barrier semaphores. Data moves between devices by JAX's collectives and lax.ppermute only.
A program may use at most 64 MiB of HBM per device.

v0:
```python
from functools import partial
import jax
import jax.numpy as jnp
from jax import lax
from jax.sharding import PartitionSpec as P

CATALOG = 2812281


def from_behind(block, axis, distance):
    devices = range(lax.axis_size(axis))
    route = [((i - distance) % len(devices), i) for i in devices]
    return lax.ppermute(block, axis, route)


def expected_log(rank_ids, sampled):
    rank_float = rank_ids.astype(jnp.float32)
    return (
        jnp.log(jnp.float32(sampled))
        + jnp.log(jnp.log1p(1.0 / (rank_float + 1.0)))
        - jnp.log(jnp.log(jnp.float32(CATALOG) + 1.0))
    )


def absorb(row_state, logits):
    run_max, run_sum = row_state
    new_max = jnp.maximum(run_max, jnp.max(logits, axis=1))
    run_sum = run_sum * jnp.exp(run_max - new_max) + jnp.sum(
        jnp.exp(logits - new_max[:, None]), axis=1
    )
    return (new_max, run_sum)


def local(documents, label_weight, sample_ids, positive_cols, up_weight, down_weight):
    wide_count = lax.axis_size("wide")
    narrow_count = lax.axis_size("narrow")
    wide_place = lax.axis_index("wide")
    narrow_place = lax.axis_index("narrow")
    lab_rows, model_width = label_weight.shape
    doc_rows = documents.shape[0]
    sampled = lab_rows * wide_count * narrow_count
    contract_rows = (((1,), (1,)), ((), ()))
    contract_first = (((0,), (0,)), ((), ()))
    pre_act = jnp.dot(documents, up_weight, preferred_element_type=jnp.float32)
    hidden = jax.nn.gelu(pre_act, approximate=False).astype(jnp.bfloat16)
    partial_out = jnp.dot(hidden, down_weight, preferred_element_type=jnp.float32)
    summed = lax.psum(partial_out, "narrow")
    embedding = (documents.astype(jnp.float32) + summed).astype(jnp.bfloat16)
    all_ranks = lax.all_gather(sample_ids, "wide", axis=0, tiled=True)
    log_expect = expected_log(all_ranks, sampled).reshape(wide_count, lab_rows)
    offsets = jnp.arange(lab_rows, dtype=jnp.int32)

    def block_logits(label_block, log_part):
        return (
            lax.dot_general(
                embedding, label_block, contract_rows, preferred_element_type=jnp.float32
            )
            - log_part[None, :]
        )

    start_state = (
        jnp.full((doc_rows,), -jnp.inf, jnp.float32),
        jnp.zeros((doc_rows,), jnp.float32),
    )
    stored_blocks = jnp.zeros((wide_count, lab_rows, model_width), jnp.bfloat16)

    def visit_block(source, label_block, carry):
        stored, row_state = carry
        stored = lax.dynamic_update_index_in_dim(stored, label_block, source, 0)
        return (stored, absorb(row_state, block_logits(label_block, log_expect[source])))

    def travel(cycle_step, carry):
        label_block, stored, row_state = carry
        source = (wide_place - cycle_step) % wide_count
        stored, row_state = visit_block(source, label_block, (stored, row_state))
        label_block = from_behind(label_block, "wide", 1)
        return (label_block, stored, row_state)

    label_block, stored_blocks, row_state = lax.fori_loop(
        0, wide_count - 1, travel, (label_weight, stored_blocks, start_state)
    )
    stored_blocks, row_state = visit_block(
        (wide_place + 1) % wide_count, label_block, (stored_blocks, row_state)
    )
    run_max, run_sum = row_state
    row_top = lax.pmax(run_max, "narrow")
    row_total = lax.psum(run_sum * jnp.exp(run_max - row_top), "narrow")
    log_total = row_top + jnp.log(row_total)
    per_doc = positive_cols.shape[1]

    def gradient_block(source):
        label_block = stored_blocks[source]
        logits = block_logits(label_block, log_expect[source])
        columns = (source * narrow_count + narrow_place) * lab_rows + offsets
        positive_hits = jnp.sum(
            (positive_cols[:, :, None] == columns[None, None, :]).astype(jnp.float32), axis=1
        )
        grad_logits = (jnp.exp(logits - log_total[:, None]) - positive_hits / per_doc).astype(
            jnp.bfloat16
        )
        return (label_block, grad_logits)

    zero_docs = jnp.zeros((doc_rows, model_width), jnp.float32)

    def carry_home(cycle_step, carry):
        home_sum, embed_back = carry
        source = (wide_place - cycle_step - 1) % wide_count
        label_block, grad_logits = gradient_block(source)
        home_sum = home_sum + lax.dot_general(
            grad_logits, embedding, contract_first, preferred_element_type=jnp.float32
        )
        embed_back = embed_back + jnp.dot(
            grad_logits, label_block, preferred_element_type=jnp.float32
        )
        home_sum = from_behind(home_sum, "wide", 1)
        return (home_sum, embed_back)

    home_sum, embed_back = lax.fori_loop(
        0, wide_count - 1, carry_home, (jnp.zeros((lab_rows, model_width), jnp.float32), zero_docs)
    )
    label_block, grad_logits = gradient_block(wide_place)
    label_grad = home_sum + lax.dot_general(
        grad_logits, embedding, contract_first, preferred_element_type=jnp.float32
    )
    embed_back = embed_back + jnp.dot(grad_logits, label_block, preferred_element_type=jnp.float32)
    embed_grad = lax.psum(embed_back, "narrow").astype(jnp.bfloat16)
    act_grad = lax.dot_general(
        embed_grad, down_weight, contract_rows, preferred_element_type=jnp.float32
    )
    _, gelu_pull = jax.vjp(partial(jax.nn.gelu, approximate=False), pre_act)
    pre_grad = gelu_pull(act_grad)[0].astype(jnp.bfloat16)
    down_term = lax.dot_general(
        hidden, embed_grad, contract_first, preferred_element_type=jnp.float32
    )
    down_grad = lax.psum_scatter(down_term, "wide", scatter_dimension=1, tiled=True)
    up_grad = lax.psum_scatter(
        lax.dot_general(
            documents, pre_grad, contract_first, preferred_element_type=jnp.float32
        ).astype(jnp.bfloat16),
        "wide",
        scatter_dimension=0,
        tiled=True,
    ).astype(jnp.float32)
    return (label_grad, up_grad, down_grad)


def solution(mesh):
    in_specs = (
        P("wide", None),
        P(("wide", "narrow"), None),
        P(("wide", "narrow")),
        P("wide", None),
        P(None, "narrow"),
        P("narrow", None),
    )
    out_specs = (P(("wide", "narrow"), None), P("wide", "narrow"), P("narrow", "wide"))
    return jax.shard_map(local, mesh=mesh, in_specs=in_specs, out_specs=out_specs, check_vma=False)
```

profile of v0, /device:TPU:2, one launch (start us, length us, event | category | flops | bytes accessed | tf_op | source)
XLA Modules:
  0.0 886.5 jit_solution(16799616201651053948)
XLA Ops:
  14.6 21.3 %all-gather = s32[16,1,128]{2,1,0:T(1,128)S(1)} all-gather(s32[1,1,128]{2,1,0:T(1,128)S(1)} %bitcast.87), channel_id=1, replica_groups=mesh['wide'=16,'narrow'=16] {'wide'}, dimensions={0}, use_global_device_ids=true | all-gather | bytes 8704 | tf_op jit(solution)/shard_map/all_gather | solution.py:49
  36.8 143.4 %all-reduce.3.cloned.1.call-done = f32[1024,768]{1,0:T(8,128)} async-done(((f32[1024,768]{1,0:T(8,128)}), f32[1024,768]{1,0:T(8,128)}) %all-reduce.3.cloned.1.call-update) | async-done | bytes 3145744 | tf_op jit(solution)/shard_map/psum | solution.py:47
  184.9 119.8 %while.40 = (s32[]{:T(128)}, bf16[128,768]{1,0:T(8,128)(2,1)S(1)}, bf16[16,128,768]{2,1,0:T(8,128)(2,1)}, f32[1024]{0:T(1024)S(1)}, f32[1024]{0:T(1024)S(1)}, /*...) while((s32[]{:T(128)}, bf16[128,768]{1,0:T(8,128)(2,1)S(1)}, ...), condition=%wide.region_4.5_spmd.clone, body=%wide.region_1.4_spmd.clone.sunk | while | flops 201856016 | bytes 4446027 | solution.py:79
  209.5 7.1 collective-permute-done
  218.3 7.2 collective-permute-done
  227.1 7.1 collective-permute-done
  235.9 7.2 collective-permute-done
  244.7 7.2 collective-permute-done
  253.6 7.1 collective-permute-done
  262.3 7.2 collective-permute-done
  271.2 7.2 collective-permute-done
  280.0 7.2 collective-permute-done
  288.8 7.2 collective-permute-done
  297.6 7.2 collective-permute-done
  306.1 32.9 %pmax.7 = f32[1024]{0:T(1024)S(1)} all-reduce(f32[1024]{0:T(1024)S(1)} %max.15), channel_id=1, replica_groups=mesh['wide'=16,'narrow'=16] {'narrow'}, use_global_device_ids=true, to_apply=%region_6.7 | all-reduce | flops 1024 | bytes 8192 | tf_op jit(solution)/shard_map/pmax | solution.py:86
  339.1 30.6 %psum.22 = f32[1024]{0:T(1024)S(1)} all-reduce(f32[1024]{0:T(1024)S(1)} %exponential_multiply_fusion), channel_id=1, replica_groups=mesh['wide'=16,'narrow'=16] {'narrow'}, use_global_device_ids=true, to_apply=%region_8.9 | all-reduce | flops 1024 | bytes 8192 | tf_op jit(solution)/shard_map/psum | solution.py:87
  372.0 208.7 %while.41 = (s32[]{:T(128)}, f32[128,768]{1,0:T(8,128)S(1)}, f32[1024,768]{1,0:T(8,128)}, s32[]{:T(128)}, bf16[16,128,768]{2,1,0:T(8,128)(2,1)}, /*index=5*/bf16...) while((s32[]{:T(128)}, f32[128,768]{1,0:T(8,128)S(1)}, ...), condition=%wide.region_11.12_spmd.clone, body=%wide.region_9.11_spmd.clone.sunk | while | flops 607748224 | bytes 15096738 | solution.py:118
  390.0 8.4 collective-permute-done.1
  419.9 6.5 collective-permute-done.1
  433.9 6.5 collective-permute-done.1
  462.0 6.5 collective-permute-done.1
  585.0 129.1 %all-reduce.4 = bf16[1024,768]{1,0:T(8,128)(2,1)} all-reduce(f32[1024,768]{1,0:T(8,128)} %convolution_add_fusion.1), channel_id=1, replica_groups=mesh['wide'=16,'narrow'=16] {'narrow'}, use_global_device_ids=true, to_apply=%region_13.14 | all-reduce | flops 786432 | bytes 4718592 | tf_op jit(solution)/shard_map/psum | solution.py:126
  724.0 78.4 %reduce-scatter.7.cloned.1.call-done = bf16[48,192]{1,0:T(8,128)(2,1)} async-done(((bf16[768,192]{1,0:T(8,128)(2,1)}), bf16[48,192]{1,0:T(8,128)(2,1)}) %reduce-scatter.7.cloned.1.call-update) | async-done | bytes 18448
  804.0 76.0 %reduce-scatter.5.cloned.1.call-done = f32[192,48]{0,1:T(8,128)} async-done(((f32[192,768]{0,1:T(8,128)}), f32[192,48]{0,1:T(8,128)}) %reduce-scatter.5.cloned.1.call-update) | async-done | bytes 36880 | tf_op jit(solution)/shard_map/reduce_scatter | solution.py:135
  (316 shorter events, 252.1 us)
Async XLA Ops:
  7.2 173.0 %all-reduce.3.cloned.1.call-start = ((), (), s32[]{:S(2)}) async-start(), calls=%async_computation.2 | async-start | bytes 6291456 | tf_op jit(solution)/shard_map/psum | solution.py:47
  14.0 788.4 %reduce-scatter.7.cloned.1.call-start = ((), (), s32[]{:S(2)}) async-start(), calls=%async_computation.4 | async-start | bytes 417792
  216.7 8.8 collective-permute-start
  234.3 8.8 collective-permute-start
  243.1 8.8 collective-permute-start
  251.9 8.8 collective-permute-start
  260.7 8.8 collective-permute-start
  269.5 8.8 collective-permute-start
  278.3 8.8 collective-permute-start
  385.6 12.8 %collective-permute-start.1 = (f32[128,768]{1,0:T(8,128)S(1)}, f32[128,768]{1,0:T(8,128)S(1)}, u32[]{:S(2)}, u32[]{:S(2)}) collective-permute-start(f32[128,768]{1,0:T(8,128)S(1)} %convolution_add_fusion.4), channel_id=1, source_target_pairs={{240,0},{0,16},{16,32},{32,48},{48,64},{64,80},{80,96},{96,112},{1... | collective-permute-start | bytes 1179656 | tf_op jit(solution)/shard_map/while/body/eval_jaxpr/ppermute | solution.py:13
  401.5 10.9 %collective-permute-start.1 = (f32[128,768]{1,0:T(8,128)S(1)}, f32[128,768]{1,0:T(8,128)S(1)}, u32[]{:S(2)}, u32[]{:S(2)}) collective-permute-start(f32[128,768]{1,0:T(8,128)S(1)} %convolution_add_fusion.4), channel_id=1, source_target_pairs={{240,0},{0,16},{16,32},{32,48},{48,64},{64,80},{80,96},{96,112},{1... | collective-permute-start | bytes 1179656 | tf_op jit(solution)/shard_map/while/body/eval_jaxpr/ppermute | solution.py:13
  415.5 10.9 %collective-permute-start.1 = (f32[128,768]{1,0:T(8,128)S(1)}, f32[128,768]{1,0:T(8,128)S(1)}, u32[]{:S(2)}, u32[]{:S(2)}) collective-permute-start(f32[128,768]{1,0:T(8,128)S(1)} %convolution_add_fusion.4), channel_id=1, source_target_pairs={{240,0},{0,16},{16,32},{32,48},{48,64},{64,80},{80,96},{96,112},{1... | collective-permute-start | bytes 1179656 | tf_op jit(solution)/shard_map/while/body/eval_jaxpr/ppermute | solution.py:13
  429.5 10.9 %collective-permute-start.1 = (f32[128,768]{1,0:T(8,128)S(1)}, f32[128,768]{1,0:T(8,128)S(1)}, u32[]{:S(2)}, u32[]{:S(2)}) collective-permute-start(f32[128,768]{1,0:T(8,128)S(1)} %convolution_add_fusion.4), channel_id=1, source_target_pairs={{240,0},{0,16},{16,32},{32,48},{48,64},{64,80},{80,96},{96,112},{1... | collective-permute-start | bytes 1179656 | tf_op jit(solution)/shard_map/while/body/eval_jaxpr/ppermute | solution.py:13
  443.6 10.9 %collective-permute-start.1 = (f32[128,768]{1,0:T(8,128)S(1)}, f32[128,768]{1,0:T(8,128)S(1)}, u32[]{:S(2)}, u32[]{:S(2)}) collective-permute-start(f32[128,768]{1,0:T(8,128)S(1)} %convolution_add_fusion.4), channel_id=1, source_target_pairs={{240,0},{0,16},{16,32},{32,48},{48,64},{64,80},{80,96},{96,112},{1... | collective-permute-start | bytes 1179656 | tf_op jit(solution)/shard_map/while/body/eval_jaxpr/ppermute | solution.py:13
  457.6 10.9 %collective-permute-start.1 = (f32[128,768]{1,0:T(8,128)S(1)}, f32[128,768]{1,0:T(8,128)S(1)}, u32[]{:S(2)}, u32[]{:S(2)}) collective-permute-start(f32[128,768]{1,0:T(8,128)S(1)} %convolution_add_fusion.4), channel_id=1, source_target_pairs={{240,0},{0,16},{16,32},{32,48},{48,64},{64,80},{80,96},{96,112},{1... | collective-permute-start | bytes 1179656 | tf_op jit(solution)/shard_map/while/body/eval_jaxpr/ppermute | solution.py:13
  471.6 10.9 %collective-permute-start.1 = (f32[128,768]{1,0:T(8,128)S(1)}, f32[128,768]{1,0:T(8,128)S(1)}, u32[]{:S(2)}, u32[]{:S(2)}) collective-permute-start(f32[128,768]{1,0:T(8,128)S(1)} %convolution_add_fusion.4), channel_id=1, source_target_pairs={{240,0},{0,16},{16,32},{32,48},{48,64},{64,80},{80,96},{96,112},{1... | collective-permute-start | bytes 1179656 | tf_op jit(solution)/shard_map/while/body/eval_jaxpr/ppermute | solution.py:13
  485.6 10.9 %collective-permute-start.1 = (f32[128,768]{1,0:T(8,128)S(1)}, f32[128,768]{1,0:T(8,128)S(1)}, u32[]{:S(2)}, u32[]{:S(2)}) collective-permute-start(f32[128,768]{1,0:T(8,128)S(1)} %convolution_add_fusion.4), channel_id=1, source_target_pairs={{240,0},{0,16},{16,32},{32,48},{48,64},{64,80},{80,96},{96,112},{1... | collective-permute-start | bytes 1179656 | tf_op jit(solution)/shard_map/while/body/eval_jaxpr/ppermute | solution.py:13
  499.6 10.9 %collective-permute-start.1 = (f32[128,768]{1,0:T(8,128)S(1)}, f32[128,768]{1,0:T(8,128)S(1)}, u32[]{:S(2)}, u32[]{:S(2)}) collective-permute-start(f32[128,768]{1,0:T(8,128)S(1)} %convolution_add_fusion.4), channel_id=1, source_target_pairs={{240,0},{0,16},{16,32},{32,48},{48,64},{64,80},{80,96},{96,112},{1... | collective-permute-start | bytes 1179656 | tf_op jit(solution)/shard_map/while/body/eval_jaxpr/ppermute | solution.py:13
  513.7 10.9 %collective-permute-start.1 = (f32[128,768]{1,0:T(8,128)S(1)}, f32[128,768]{1,0:T(8,128)S(1)}, u32[]{:S(2)}, u32[]{:S(2)}) collective-permute-start(f32[128,768]{1,0:T(8,128)S(1)} %convolution_add_fusion.4), channel_id=1, source_target_pairs={{240,0},{0,16},{16,32},{32,48},{48,64},{64,80},{80,96},{96,112},{1... | collective-permute-start | bytes 1179656 | tf_op jit(solution)/shard_map/while/body/eval_jaxpr/ppermute | solution.py:13
  527.7 10.9 %collective-permute-start.1 = (f32[128,768]{1,0:T(8,128)S(1)}, f32[128,768]{1,0:T(8,128)S(1)}, u32[]{:S(2)}, u32[]{:S(2)}) collective-permute-start(f32[128,768]{1,0:T(8,128)S(1)} %convolution_add_fusion.4), channel_id=1, source_target_pairs={{240,0},{0,16},{16,32},{32,48},{48,64},{64,80},{80,96},{96,112},{1... | collective-permute-start | bytes 1179656 | tf_op jit(solution)/shard_map/while/body/eval_jaxpr/ppermute | solution.py:13
  541.7 10.9 %collective-permute-start.1 = (f32[128,768]{1,0:T(8,128)S(1)}, f32[128,768]{1,0:T(8,128)S(1)}, u32[]{:S(2)}, u32[]{:S(2)}) collective-permute-start(f32[128,768]{1,0:T(8,128)S(1)} %convolution_add_fusion.4), channel_id=1, source_target_pairs={{240,0},{0,16},{16,32},{32,48},{48,64},{64,80},{80,96},{96,112},{1... | collective-permute-start | bytes 1179656 | tf_op jit(solution)/shard_map/while/body/eval_jaxpr/ppermute | solution.py:13
  555.7 10.9 %collective-permute-start.1 = (f32[128,768]{1,0:T(8,128)S(1)}, f32[128,768]{1,0:T(8,128)S(1)}, u32[]{:S(2)}, u32[]{:S(2)}) collective-permute-start(f32[128,768]{1,0:T(8,128)S(1)} %convolution_add_fusion.4), channel_id=1, source_target_pairs={{240,0},{0,16},{16,32},{32,48},{48,64},{64,80},{80,96},{96,112},{1... | collective-permute-start | bytes 1179656 | tf_op jit(solution)/shard_map/while/body/eval_jaxpr/ppermute | solution.py:13
  569.7 10.9 %collective-permute-start.1 = (f32[128,768]{1,0:T(8,128)S(1)}, f32[128,768]{1,0:T(8,128)S(1)}, u32[]{:S(2)}, u32[]{:S(2)}) collective-permute-start(f32[128,768]{1,0:T(8,128)S(1)} %convolution_add_fusion.4), channel_id=1, source_target_pairs={{240,0},{0,16},{16,32},{32,48},{48,64},{64,80},{80,96},{96,112},{1... | collective-permute-start | bytes 1179656 | tf_op jit(solution)/shard_map/while/body/eval_jaxpr/ppermute | solution.py:13
  719.7 160.3 %reduce-scatter.5.cloned.1.call-start = ((), (), s32[]{:S(2)}) async-start(), calls=%async_computation.3 | async-start | bytes 835584 | tf_op jit(solution)/shard_map/reduce_scatter | solution.py:135
  (16 other events, 105.6 us)
Sparse Core Ops, SparseCore 0:
  14.1 166.0 all-reduce.2
  719.8 82.5 reduce-scatter.6
  807.0 72.8 reduce-scatter.4
where the time goes:
time: 888 us; the launch traced here: 886 us
  waiting for transfers between devices  490 us (55%)
  blocking collectives  214 us (24%)
  matrix products  126 us (14%)
  local copies, waits for them, and re-layouts  19.7 us (2%)
  other arithmetic  18.7 us (2%)
  between operations  13.9 us (2%)
    ppermute x30, waiting for transfers between devices, from_behind(): return lax.ppermute(block, axis, route)  192 us
    psum x1, waiting for transfers between devices, local(): summed = lax.psum(partial_out, 'narrow')  143 us
    psum x1, blocking collectives, local(): embed_grad = lax.psum(embed_back, 'narrow').astype(jnp.bfloat16)  129 us
    unnamed x4, waiting for transfers between devices  78.5 us
    reduce_scatter x1, waiting for transfers between devices, local(): lax.psum_scatter(down_term, 'wide', scatter_dimension=1, tiled=True)  76 us
    dot_general x15, matrix products, carry_home(): jnp.dot(grad_logits, label_block, preferred_element_type=jnp.float32)  63.1 us
    dot_general x32, matrix products, block_logits(): lax.dot_general(embedding, label_block, contract_rows, preferred_element_...  36.8 us
    pmax x1, blocking collectives, local(): row_top = lax.pmax(run_max, 'narrow')  32.9 us
  transfers between devices with their start and end apart: 33, of which 33 were waited for; matrix products, arithmetic and copies ran while one was open for 10% of the time, Pallas kernels for 0%

commit v1 on v0

--- a/solution.py
+++ b/solution.py
@@ -1,3 +1,4 @@
+import functools
 from functools import partial
 import jax
 import jax.numpy as jnp
@@ -5,6 +6,14 @@
 from jax.sharding import PartitionSpec as P
 
 CATALOG = 2812281
+
+
+def manage_the_axis_part(x_in, peer_axis):
+    right_arr = lax.all_gather(x_in, peer_axis).sum(axis=0)
+    return right_arr
+
+
+_time_slices = functools.partial(manage_the_axis_part, peer_axis="narrow")
 
 
 def from_behind(block, axis, distance):
@@ -44,7 +53,7 @@
     pre_act = jnp.dot(documents, up_weight, preferred_element_type=jnp.float32)
     hidden = jax.nn.gelu(pre_act, approximate=False).astype(jnp.bfloat16)
     partial_out = jnp.dot(hidden, down_weight, preferred_element_type=jnp.float32)
-    summed = lax.psum(partial_out, "narrow")
+    summed = _time_slices(partial_out)
     embedding = (documents.astype(jnp.float32) + summed).astype(jnp.bfloat16)
     all_ranks = lax.all_gather(sample_ids, "wide", axis=0, tiled=True)
     log_expect = expected_log(all_ranks, sampled).reshape(wide_count, lab_rows)

time: 888 us -> 1770 us (1.99)
  waiting for transfers between devices: 490 us -> 1350 us
  other arithmetic: 18.7 us -> 38.2 us
    all_gather x0 -> x1, waiting for transfers between devices: none -> 1010 us  [manage_the_axis_part(): right_arr = lax.all_gather(x_in, peer_axis).sum(axis=0)]
    psum x1 -> x0, waiting for transfers between devices: 143 us -> none  [local(): summed = lax.psum(partial_out, 'narrow')]
    reduce_sum x0 -> x1, other arithmetic: none -> 19.5 us  [manage_the_axis_part(): right_arr = lax.all_gather(x_in, peer_axis).sum(axis=0)]
  transfers between devices with their start and end apart: 33 -> 33, of which waited for: 33 -> 33; matrix products, arithmetic and copies ran while one was open for 10% -> 5% of each run, Pallas kernels for 0% -> 0%
where the time goes in v1:
time: 1770 us
  waiting for transfers between devices  1350 us (76%)
  blocking collectives  214 us (12%)
  matrix products  125 us (7%)
  other arithmetic  38.2 us (2%)
  local copies, waits for them, and re-layouts  20.4 us (1%)
    all_gather x1, waiting for transfers between devices, manage_the_axis_part(): right_arr = lax.all_gather(x_in, peer_axis).sum(axis=0)  1010 us
    ppermute x30, waiting for transfers between devices, from_behind(): return lax.ppermute(block, axis, route)  193 us
    psum x1, blocking collectives, local(): embed_grad = lax.psum(embed_back, 'narrow').astype(jnp.bfloat16)  129 us
    unnamed x4, waiting for transfers between devices  78.9 us
    reduce_scatter x1, waiting for transfers between devices, local(): lax.psum_scatter(down_term, 'wide', scatter_dimension=1, tiled=True)  76 us
    dot_general x15, matrix products, carry_home(): jnp.dot(grad_logits, label_block, preferred_element_type=jnp.float32)  62.4 us
    dot_general x32, matrix products, block_logits(): lax.dot_general(embedding, label_block, contract_rows, preferred_element_...  36.8 us
  transfers between devices with their start and end apart: 33, of which 33 were waited for; matrix products, arithmetic and copies ran while one was open for 5% of the time, Pallas kernels for 0%

profile of v1, /device:TPU:2, one launch (start us, length us, event | category | flops | bytes accessed | tf_op | source)
XLA Modules:
  0.0 1769.2 jit_solution(12904130135525270723)
XLA Ops:
  15.3 21.3 %all-gather.1 = s32[16,1,128]{2,1,0:T(1,128)S(1)} all-gather(s32[1,1,128]{2,1,0:T(1,128)S(1)} %bitcast.89), channel_id=1, replica_groups=mesh['wide'=16,'narrow'=16] {'wide'}, dimensions={0}, use_global_device_ids=true | all-gather | bytes 8704 | tf_op jit(solution)/shard_map/all_gather | solution.py:58
  37.5 1005.3 %all-gather.4.cloned.1.call-done = f32[16384,768]{1,0:T(8,128)} async-done(((f32[1024,768]{1,0:T(8,128)}), f32[16384,768]{1,0:T(8,128)}) %all-gather.4.cloned.1.call-update) | async-done | bytes 50331664 | tf_op jit(solution)/shard_map/all_gather | solution.py:12
  1042.9 19.5 %reduce_sum.59 = f32[1024,768]{1,0:T(8,128)} reduce(f32[16,1024,768]{2,1,0:T(8,128)} %bitcast.87, f32[]{:T(128)} %constant.204.clone.1), dimensions={0}, to_apply=%region_0.0 | reduce | flops 11796480 | bytes 53477380 | tf_op jit(solution)/shard_map/reduce_sum | solution.py:12
  1067.0 119.6 %while.40 = (s32[]{:T(128)}, bf16[128,768]{1,0:T(8,128)(2,1)S(1)}, bf16[16,128,768]{2,1,0:T(8,128)(2,1)}, f32[1024]{0:T(1024)S(1)}, f32[1024]{0:T(1024)S(1)}, /*...) while((s32[]{:T(128)}, bf16[128,768]{1,0:T(8,128)(2,1)S(1)}, ...), condition=%wide.region_4.5_spmd.clone, body=%wide.region_1.4_spmd.clone.sunk | while | flops 201856016 | bytes 4446027 | solution.py:88
  1091.5 7.2 collective-permute-done
  1100.3 7.2 collective-permute-done
  1109.1 7.2 collective-permute-done
  1117.9 7.1 collective-permute-done
  1126.7 7.2 collective-permute-done
  1135.5 7.2 collective-permute-done
  1144.3 7.2 collective-permute-done
  1153.1 7.1 collective-permute-done
  1161.9 7.2 collective-permute-done
  1170.7 7.2 collective-permute-done
  1179.5 7.2 collective-permute-done
  1187.3 33.1 %pmax.7 = f32[1024]{0:T(1024)S(1)} all-reduce(f32[1024]{0:T(1024)S(1)} %max.15), channel_id=1, replica_groups=mesh['wide'=16,'narrow'=16] {'narrow'}, use_global_device_ids=true, to_apply=%region_6.7 | all-reduce | flops 1024 | bytes 8192 | tf_op jit(solution)/shard_map/pmax | solution.py:95
  1220.6 30.8 %psum.14 = f32[1024]{0:T(1024)S(1)} all-reduce(f32[1024]{0:T(1024)S(1)} %exponential_multiply_fusion), channel_id=1, replica_groups=mesh['wide'=16,'narrow'=16] {'narrow'}, use_global_device_ids=true, to_apply=%region_8.9 | all-reduce | flops 1024 | bytes 8192 | tf_op jit(solution)/shard_map/psum | solution.py:96
  1254.3 208.6 %while.41 = (s32[]{:T(128)}, f32[128,768]{1,0:T(8,128)S(1)}, f32[1024,768]{1,0:T(8,128)}, s32[]{:T(128)}, bf16[16,128,768]{2,1,0:T(8,128)(2,1)}, /*index=5*/bf16...) while((s32[]{:T(128)}, f32[128,768]{1,0:T(8,128)S(1)}, ...), condition=%wide.region_11.12_spmd.clone, body=%wide.region_9.11_spmd.clone.sunk | while | flops 607748224 | bytes 15096738 | solution.py:127
  1272.2 8.4 collective-permute-done.1
  1316.1 6.6 collective-permute-done.1
  1344.1 6.6 collective-permute-done.1
  1467.2 129.0 %all-reduce.1 = bf16[1024,768]{1,0:T(8,128)(2,1)} all-reduce(f32[1024,768]{1,0:T(8,128)} %convolution_add_fusion.1), channel_id=1, replica_groups=mesh['wide'=16,'narrow'=16] {'narrow'}, use_global_device_ids=true, to_apply=%region_13.14 | all-reduce | flops 786432 | bytes 4718592 | tf_op jit(solution)/shard_map/psum | solution.py:135
  1606.2 78.9 %reduce-scatter.7.cloned.1.call-done = bf16[48,192]{1,0:T(8,128)(2,1)} async-done(((bf16[768,192]{1,0:T(8,128)(2,1)}), bf16[48,192]{1,0:T(8,128)(2,1)}) %reduce-scatter.7.cloned.1.call-update) | async-done | bytes 18448
  1686.6 76.0 %reduce-scatter.5.cloned.1.call-done = f32[192,48]{0,1:T(8,128)} async-done(((f32[192,768]{0,1:T(8,128)}), f32[192,48]{0,1:T(8,128)}) %reduce-scatter.5.cloned.1.call-update) | async-done | bytes 36880 | tf_op jit(solution)/shard_map/reduce_scatter | solution.py:144
  (317 shorter events, 259.0 us)
Async XLA Ops:
  7.2 1035.7 %all-gather.4.cloned.1.call-start = ((), (), s32[]{:S(2)}) async-start(), calls=%async_computation.3 | async-start | bytes 53477376 | tf_op jit(solution)/shard_map/all_gather | solution.py:12
  14.7 1670.3 %reduce-scatter.7.cloned.1.call-start = ((), (), s32[]{:S(2)}) async-start(), calls=%async_computation.4 | async-start | bytes 417792
  1089.8 8.8 collective-permute-start
  1107.5 8.8 collective-permute-start
  1125.1 8.8 collective-permute-start
  1142.7 8.8 collective-permute-start
  1160.3 8.8 collective-permute-start
  1169.1 8.8 collective-permute-start
  1177.9 8.8 collective-permute-start
  1267.9 12.7 collective-permute-start.1
  1283.7 10.9 collective-permute-start.1
  1297.8 10.9 collective-permute-start.1
  1311.8 10.9 collective-permute-start.1
  1325.8 10.9 collective-permute-start.1
  1339.8 10.9 collective-permute-start.1
  1353.8 10.9 collective-permute-start.1
  1367.9 10.9 collective-permute-start.1
  1381.9 10.9 collective-permute-start.1
  1395.9 10.9 collective-permute-start.1
  1409.9 10.9 collective-permute-start.1
  1423.9 10.9 collective-permute-start.1
  1438.0 10.9 collective-permute-start.1
  1452.0 10.9 collective-permute-start.1
  1601.9 160.8 %reduce-scatter.5.cloned.1.call-start = ((), (), s32[]{:S(2)}) async-start(), calls=%async_computation.2 | async-start | bytes 835584 | tf_op jit(solution)/shard_map/reduce_scatter | solution.py:144
  (16 other events, 104.6 us)
Sparse Core Ops, SparseCore 0:
  14.8 1028.0 all-gather.3
  1602.0 82.9 reduce-scatter.6
  1689.7 72.9 reduce-scatter.4
